TPU v7x, 32 devices: a whole 2x2x4 slice. The times are simulated.
32 devices in a mesh: gx: 4 (over x, core), gy: 8 (over z, y).
Axes of the slice: x: 2, y: 2, z: 4, core: 2. Of those that a mesh axis runs over, the one named last changes fastest.
Arguments:
- token_ids: int32 [192, 2], replicated, may hold values from 0 to 64127
- lengths: int32 [192], P(('gx', 'gy')), may hold values from 64 to 512, as said below
- embedding: bfloat16 [64128, 8192], P('gy', 'gx'), may hold values from -6 to 6
- norm_gain: float32 [8192], P('gx'), may hold values from 0.1 to 1.9
- qkv_weight: bfloat16 [8192, 10240], P('gx', 'gy'), may hold values from -0.0625 to 0.0625
- out_weight: bfloat16 [8192, 8192], P('gy', 'gx'), may hold values from -0.5 to 0.5
- key_cache: bfloat16 [192, 512, 1024], P(('gx', 'gy'))
- value_cache: bfloat16 [192, 512, 1024], P(('gx', 'gy')), may hold values from -6 to 6
Outputs:
- layer_out: bfloat16 [192, 2, 8192], P('gy', None, 'gx')
- new_keys: bfloat16 [192, 2, 1024], P(('gx', 'gy'))
- new_values: bfloat16 [192, 2, 1024], P(('gx', 'gy'))
Inputs may be any that keep to these rules, and one draw needn't show every extreme that they name: `lengths`: every length is at least 64 and at most 512; some sequence has exactly 512.
All inputs are finite; a program needn't handle non-finite values.
Results may differ from a plain program's by a relative error of at most 0.012.
The roundings to bfloat16 on the way count: a program that leaves them out, or rounds other values in their place, can miss the bound.
Values may be sent and summed in bfloat16 or wider, within the bound.
No kernel may reach another device: no remote copies, remote signals or barrier semaphores. Data moves between devices by JAX's collectives and lax.ppermute only.
A program may use at most 192 MiB of HBM per device.

v0:
```python
import jax
import jax.numpy as jnp
from jax import lax
from jax.sharding import PartitionSpec as P

D = 8192
HEADS = 64
KV_HEADS = 8
HEAD_DIM = 128


EPS = 1e-05


def rotate(values, positions):
    half = HEAD_DIM // 2
    freq = jnp.exp(
        -jnp.log(jnp.float32(500000.0)) * 2.0 * jnp.arange(half, dtype=jnp.float32) / HEAD_DIM
    )
    angle = positions[:, :, None, None] * freq[None, None, None, :]
    cosine = jnp.cos(angle)
    sine = jnp.sin(angle)
    lower = values[..., :half]
    upper = values[..., half:]
    return jnp.concatenate([lower * cosine - upper * sine, upper * cosine + lower * sine], axis=-1)


def attend(query, keys_new, vals_new, keys_old, vals_old, lens):
    seqs = query.shape[0]
    slots = keys_old.shape[1]
    group = HEADS // KV_HEADS
    scale = HEAD_DIM ** (-0.5)
    query_g = query.reshape(seqs, 2, KV_HEADS, group, HEAD_DIM)
    keys_c = keys_old.reshape(seqs, slots, KV_HEADS, HEAD_DIM)
    vals_c = vals_old.reshape(seqs, slots, KV_HEADS, HEAD_DIM)
    old_scores = (
        jnp.einsum("stghd,scgd->sgthc", query_g, keys_c, preferred_element_type=jnp.float32) * scale
    )
    new_scores = (
        jnp.einsum("stghd,sugd->sgthu", query_g, keys_new, preferred_element_type=jnp.float32)
        * scale
    )
    valid = jnp.arange(slots, dtype=jnp.int32)[None, :] < lens[:, None]
    old_scores = jnp.where(valid[:, None, None, None, :], old_scores, -1e30)
    causal = jnp.arange(2)[None, :] <= jnp.arange(2)[:, None]
    new_scores = jnp.where(causal[None, None, :, None, :], new_scores, -1e30)
    top = jnp.maximum(jnp.max(old_scores, axis=-1), jnp.max(new_scores, axis=-1))
    old_p = jnp.exp(old_scores - top[..., None])
    new_p = jnp.exp(new_scores - top[..., None])
    total = jnp.sum(old_p, axis=-1) + jnp.sum(new_p, axis=-1)
    summed = jnp.einsum(
        "sgthc,scgd->stghd", old_p.astype(jnp.bfloat16), vals_c, preferred_element_type=jnp.float32
    )
    summed = summed + jnp.einsum(
        "sgthu,sugd->stghd",
        new_p.astype(jnp.bfloat16),
        vals_new,
        preferred_element_type=jnp.float32,
    )
    result = summed / jnp.transpose(total, (0, 2, 1, 3))[..., None]
    return result.astype(jnp.bfloat16).reshape(seqs * 2, HEADS * HEAD_DIM)


def on_device(
    token_ids, lengths, embedding, norm_gain, qkv_weight, out_weight, key_cache, value_cache
):
    flat_ids = token_ids.reshape(-1)
    span = embedding.shape[0]
    local_ids = flat_ids - lax.axis_index("gy") * span
    inside = (local_ids >= 0) & (local_ids < span)
    picked = jnp.take(embedding, jnp.clip(local_ids, 0, span - 1), axis=0)
    picked = jnp.where(inside[:, None], picked, jnp.zeros((), picked.dtype))
    feature_cols = lax.psum(picked, "gy").astype(jnp.float32)
    power = jnp.sum(feature_cols * feature_cols, axis=1)
    scaled = (feature_cols * norm_gain[None, :]).astype(jnp.bfloat16)
    share = feature_cols.shape[0] // lax.axis_size("gx")
    total_power = lax.psum(power, "gx")
    summed = lax.psum_scatter(
        jnp.dot(scaled, qkv_weight, preferred_element_type=jnp.float32),
        "gx",
        scatter_dimension=0,
        tiled=True,
    )
    my_power = lax.dynamic_slice_in_dim(total_power, lax.axis_index("gx") * share, share, 0)
    qkv_rows = (summed * lax.rsqrt(my_power / D + EPS)[:, None]).astype(jnp.bfloat16)
    qkv_local = lax.all_to_all(qkv_rows, "gy", split_axis=0, concat_axis=1, tiled=True)
    seqs = lengths.shape[0]
    kv_width = KV_HEADS * HEAD_DIM
    query = qkv_local[:, :D].astype(jnp.float32).reshape(seqs, 2, HEADS, HEAD_DIM)
    keys = qkv_local[:, D : D + kv_width].astype(jnp.float32).reshape(seqs, 2, KV_HEADS, HEAD_DIM)
    vals = qkv_local[:, D + kv_width :].reshape(seqs, 2, KV_HEADS, HEAD_DIM)
    positions = lengths.astype(jnp.float32)[:, None] + jnp.arange(2, dtype=jnp.float32)[None, :]
    query_r = rotate(query, positions).astype(jnp.bfloat16)
    keys_r = rotate(keys, positions).astype(jnp.bfloat16)
    attended = attend(query_r, keys_r, vals, key_cache, value_cache, lengths)
    column_block = lax.all_to_all(attended, "gy", split_axis=1, concat_axis=0, tiled=True)
    partial_out = jnp.dot(
        lax.all_gather(column_block, "gx", axis=0, tiled=True),
        out_weight,
        preferred_element_type=jnp.float32,
    )
    projected = lax.psum_scatter(partial_out, "gy", scatter_dimension=0, tiled=True)
    mine = projected.shape[0]
    residual = lax.dynamic_slice_in_dim(feature_cols, lax.axis_index("gy") * mine, mine, 0)
    layer_out = (
        (residual + projected).astype(jnp.bfloat16).reshape(mine // 2, 2, projected.shape[1])
    )
    new_keys = keys_r.reshape(seqs, 2, kv_width)
    new_values = vals.reshape(seqs, 2, kv_width)
    return (layer_out, new_keys, new_values)


def solution(mesh):
    placed = (
        P(),
        P(("gx", "gy")),
        P("gy", "gx"),
        P("gx"),
        P("gx", "gy"),
        P("gy", "gx"),
        P(("gx", "gy"), None, None),
        P(("gx", "gy"), None, None),
    )
    return jax.shard_map(
        on_device,
        mesh=mesh,
        in_specs=placed,
        out_specs=(P("gy", None, "gx"), P(("gx", "gy"), None, None), P(("gx", "gy"), None, None)),
        check_vma=False,
    )
```

profile of v0, /device:TPU:0, one launch (start us, length us, event | category | flops | bytes accessed | tf_op | source)
XLA Modules:
  0.0 293.6 jit_solution(7447271493646251156)
XLA Ops:
  7.2 0.7 subtract_clamp_fusion
  8.3 0.7 compare_and_fusion
  9.4 19.8 %gather_fusion = bf16[384,2048]{1,0:T(8,128)(2,1)S(1)} fusion(bf16[8016,2048]{1,0:T(8,128)(2,1)} %param.10, s32[1024]{0:T(1024)S(1)} %pad_clamp_fusion), kind=kCustom, calls=%fused_computation | custom fusion | bytes 3147264 | tf_op jit(solution)/shard_map/jit(_take)/gather | solution.py:71
  29.2 1.4 select_select_fusion
  30.7 92.2 %all-reduce.2.cloned.1.call-done = bf16[384,2048]{1,0:T(8,128)(2,1)} async-done(((bf16[384,2048]{1,0:T(8,128)(2,1)}), bf16[384,2048]{1,0:T(8,128)(2,1)}) %all-reduce.2.cloned.1.call-update) | async-done | bytes 1572880 | tf_op jit(solution)/shard_map/psum | solution.py:73
  123.0 6.4 %fusion.4 = f32[384,1280]{1,0:T(8,128)} fusion(bf16[2048,1280]{1,0:T(8,128)(2,1)} %param.12, f32[2048]{0:T(1024)S(1)} %copy-done.2, bf16[384,2048]{1,0:T(8,128)(2,1)} %all-reduce.2.cloned.1.call-done), kind=kOutput, calls=%fused_computation.9 | convolution fusion | flops 2015625216 | bytes 8790016 | tf_op jit(solution)/shard_map/dot_general | solution.py:79
  129.5 7.3 %copy.56 = bf16[384,8,8,128]{3,2,1,0:T(8,128)(2,1)} copy(bf16[384,8,8,128]{3,1,2,0:T(8,128)(2,1)} %bitcast.71) | data formatting | bytes 12582912
  136.7 4.3 %copy.58 = bf16[384,8,8,128]{3,2,1,0:T(8,128)(2,1)} copy(bf16[384,8,8,128]{3,1,2,0:T(8,128)(2,1)S(1)} %bitcast.74) | data formatting | bytes 12582912
  141.4 6.0 %bitcast_bitcast_fusion.1 = bf16[6,512,8,128,1]{3,2,1,0,4:T(8,128)(2,1)} fusion(bf16[6,512,8,128]{3,2,1,0:T(8,128)(2,1)} %bitcast.70), kind=kLoop, calls=%fused_computation.2 | loop fusion | bytes 12582912 | tf_op jit(solution)/shard_map/reshape | solution.py:34
  147.3 0.4 multiply_reduce_fusion
  147.7 7.4 %psum.15 = f32[384]{0:T(512)S(1)} all-reduce(f32[384]{0:T(512)S(1)} %multiply_reduce_fusion), channel_id=1, replica_groups=mesh['gx'=4,'gy'=8] {'gx'}, use_global_device_ids=true, to_apply=%region_3.4 | all-reduce | flops 384 | bytes 3072 | tf_op jit(solution)/shard_map/psum | solution.py:77
  155.2 4.1 %reduce-scatter.3.cloned.1.call-done = f32[96,1280]{1,0:T(8,128)} async-done(((f32[384,1280]{1,0:T(8,128)}), f32[96,1280]{1,0:T(8,128)}) %reduce-scatter.3.cloned.1.call-update) | async-done | bytes 491536 | tf_op jit(solution)/shard_map/reduce_scatter | solution.py:78
  159.3 1.1 multiply_convert_fusion.2
  160.5 0.8 all_to_all.28
  161.3 5.5 %all-to-all-start = ((bf16[8,12,1280]{2,1,0:T(8,128)(2,1)}), bf16[8,12,1280]{2,1,0:T(8,128)(2,1)S(1)}, u32[]{:S(2)}, u32[]{:S(2)}) async-start(bf16[8,12,1280]{2,1,0:T(8,128)(2,1)} %all_to_all.28), calls=%async_computation.1 | async-start | bytes 655360 | tf_op jit(solution)/shard_map/all_to_all | solution.py:86
  166.8 0.2 reduce-scatter.5.cloned.1.call-start
  167.0 5.8 %bitcast_bitcast_fusion = bf16[6,512,8,128,1]{3,2,1,0,4:T(8,128)(2,1)} fusion(bf16[6,512,8,128]{3,2,1,0:T(8,128)(2,1)} %bitcast.69), kind=kLoop, calls=%fused_computation.1 | loop fusion | bytes 12582912 | tf_op jit(solution)/shard_map/reshape | solution.py:35
  172.8 4.1 %all-to-all-done = bf16[8,12,1280]{2,1,0:T(8,128)(2,1)S(1)} async-done(((bf16[8,12,1280]{2,1,0:T(8,128)(2,1)}), bf16[8,12,1280]{2,1,0:T(8,128)(2,1)S(1)}, u32[]{:S(2)}, u32[]{:S(2)}) %all-to-all-start) | async-done | bytes 245792 | tf_op jit(solution)/shard_map/all_to_all | solution.py:86
  177.7 4.9 %fusion.33 = (f32[6,8,2,8]{3,2,1,0:T(2,128)S(1)}, f32[6,8,2,8,512]{4,3,2,1,0:T(8,128)S(1)}) fusion(bf16[6,512,8,128,1]{3,2,1,0,4:T(8,128)(2,1)} %bitcast_bitcast_fusion.1, pred[6,512]{1,0:T(8,128)(4,1)S(1)} %iota_compare_fusion, bf16[6,2,8,8,64]{4,3,2,1,0:T(8,128)(2,1)S(1)} %get-tuple-element.4, bf16[6,2,8,8,64]{4,3,2,1,0:T(8,128)(2,1)S(1)} %get-tuple-element.3), kind=kOutput, calls=%fused_computation.62 | convolution fusion | flops 102235392 | bytes 8067072 | tf_op jit(solution)/shard_map/stghd,scgd->sgthc/dot_general | solution.py:37
  182.6 1.1 fusion.34
  183.9 0.6 fusion.9
  184.6 1.3 fusion.13
  185.9 0.3 fusion.16
  186.4 11.9 %all_to_all.38 = bf16[12,8,1024]{2,0,1:T(8,128)(2,1)S(1)} all-to-all(bf16[12,8,1024]{2,0,1:T(8,128)(2,1)S(1)} %reshape.193), channel_id=1, replica_groups=mesh['gx'=4,'gy'=8] {'gy'}, dimensions={1} | all-to-all | bytes 393216 | tf_op jit(solution)/shard_map/all_to_all | solution.py:96
  198.4 7.7 %all_gather.3 = bf16[384,1024]{1,0:T(8,128)(2,1)S(1)} all-gather(bf16[96,1024]{1,0:T(8,128)(2,1)S(1)} %all_to_all.35), channel_id=1, replica_groups=mesh['gx'=4,'gy'=8] {'gx'}, dimensions={0}, use_global_device_ids=true | all-gather | bytes 983040 | tf_op jit(solution)/shard_map/all_gather | solution.py:98
  206.1 5.7 %fusion.35 = f32[384,2048]{1,0:T(8,128)} fusion(bf16[384,1024]{1,0:T(8,128)(2,1)S(1)} %all_gather.3, bf16[1024,2048]{1,0:T(8,128)(2,1)} %param.13), kind=kOutput, calls=%fused_computation.64 | convolution fusion | flops 1610612736 | bytes 8126464 | tf_op jit(solution)/shard_map/dot_general | solution.py:97
  211.7 2.1 convert_element_type.35
  213.8 0.6 reshape_reshape.3
  214.4 0.7 fusion.39
  215.2 70.0 %reduce-scatter.5.cloned.1.call-done = f32[48,2048]{1,0:T(8,128)} async-done(((f32[384,2048]{1,0:T(8,128)}), f32[48,2048]{1,0:T(8,128)}) %reduce-scatter.5.cloned.1.call-update) | async-done | bytes 393232 | tf_op jit(solution)/shard_map/reduce_scatter | solution.py:102
  285.1 1.2 add_convert_fusion
  286.3 0.8 reshape.176
  (56 shorter events, 2.5 us)
Async XLA Ops:
  7.2 115.8 %all-reduce.2.cloned.1.call-start = ((), (), s32[]{:S(2)}) async-start(), calls=%async_computation.4 | async-start | bytes 3145728 | tf_op jit(solution)/shard_map/psum | solution.py:73
  29.2 93.8 %copy-start.2 = (f32[2048]{0:T(1024)S(1)}, f32[2048]{0:T(1024)}, u32[]{:S(2)}) copy-start(f32[2048]{0:T(1024)} %param.11) | copy-start | bytes 24580
  30.7 98.8 %copy-start.1 = (s32[6]{0:T(128)S(1)}, s32[6]{0:T(128)}, u32[]{:S(2)}) copy-start(s32[6]{0:T(128)} %param.9) | copy-start | bytes 76
  30.7 128.7 %reduce-scatter.3.cloned.1.call-start = ((), (), s32[]{:S(2)}) async-start(), calls=%async_computation.5 | async-start | bytes 2457600 | tf_op jit(solution)/shard_map/reduce_scatter | solution.py:78
  129.4 7.3 %slice-start.2 = ((s8[6291456]{0:T(1024)(128)(4,1)}), s8[2097152]{0:T(1024)(128)(4,1)S(1)}, s32[]{:S(2)}) async-start(s8[6291456]{0:T(1024)(128)(4,1)} %bitcast.72), calls=%async_computation.9 | async-start | bytes 4194304
  129.5 7.3 %slice-start.3 = ((s8[6291456]{0:T(1024)(128)(4,1)}), s8[4194304]{0:T(1024)(128)(4,1)S(1)}, s32[]{:S(2)}) async-start(s8[6291456]{0:T(1024)(128)(4,1)} %bitcast.72), calls=%async_computation.10 | async-start | bytes 8388608
  141.4 6.0 %copy-start = (bf16[384,2048]{1,0:T(8,128)(2,1)S(1)}, bf16[384,2048]{1,0:T(8,128)(2,1)}, u32[]{:S(2)}) copy-start(bf16[384,2048]{1,0:T(8,128)(2,1)} %all-reduce.2.cloned.1.call-done) | copy-start | bytes 4718596
  161.3 15.7 %all-to-all-start = ((bf16[8,12,1280]{2,1,0:T(8,128)(2,1)}), bf16[8,12,1280]{2,1,0:T(8,128)(2,1)S(1)}, u32[]{:S(2)}, u32[]{:S(2)}) async-start(bf16[8,12,1280]{2,1,0:T(8,128)(2,1)} %all_to_all.28), calls=%async_computation.1 | async-start | bytes 655360 | tf_op jit(solution)/shard_map/all_to_all | solution.py:86
  166.8 118.3 %reduce-scatter.5.cloned.1.call-start = ((), (), s32[]{:S(2)}) async-start(), calls=%async_computation.6 | async-start | bytes 3538944 | tf_op jit(solution)/shard_map/reduce_scatter | solution.py:102
  177.5 7.1 %slice-start = ((s8[6291456]{0:T(1024)(128)(4,1)}), s8[4194304]{0:T(1024)(128)(4,1)S(1)}, s32[]{:S(2)}) async-start(s8[6291456]{0:T(1024)(128)(4,1)} %bitcast.67), calls=%async_computation.7 | async-start | bytes 8388608
  177.7 6.8 %slice-start.1 = ((s8[6291456]{0:T(1024)(128)(4,1)}), s8[2097152]{0:T(1024)(128)(4,1)S(1)}, s32[]{:S(2)}) async-start(s8[6291456]{0:T(1024)(128)(4,1)} %bitcast.67), calls=%async_computation.8 | async-start | bytes 4194304
Sparse Core Ops, SparseCore 0:
  30.8 92.1 all-reduce.1
  129.5 29.7 reduce-scatter.2
  211.9 73.2 reduce-scatter.4
where the time goes:
time: 294 us
  waiting for transfers between devices  171 us (58%)
  local copies, waits for them, and re-layouts  46.8 us (16%)
  blocking collectives  27 us (9%)
  matrix products  19.6 us (7%)
  between operations  14.1 us (5%)
  other arithmetic  9.86 us (3%)
  starting transfers between devices  5.83 us (2%)
    psum x1, waiting for transfers between devices, on_device(): feature_cols = lax.psum(picked, 'gy').astype(jnp.float32)  92.2 us
    reduce_scatter x1, waiting for transfers between devices, on_device(): lax.psum_scatter(partial_out, 'gy', scatter_dimension=0, tiled=True)  70 us
    gather x1, local copies, waits for them, and re-layouts, on_device(): picked = jnp.take(embedding, jnp.clip(local_ids, 0, span - 1), axis=0)  19.8 us
    all_to_all x1, blocking collectives, on_device(): lax.all_to_all(attended, 'gy', split_axis=1, concat_axis=0, tiled=True)  11.9 us
    unnamed x24, local copies, waits for them, and re-layouts  11.8 us
    all_gather x1, blocking collectives, on_device(): lax.all_gather(column_block, 'gx', axis=0, tiled=True)  7.66 us
    psum x1, blocking collectives, on_device(): total_power = lax.psum(power, 'gx')  7.4 us
    dot_general x1, matrix products, on_device(): jnp.dot(scaled, qkv_weight, preferred_element_type=jnp.float32)  6.44 us
  transfers between devices with their start and end apart: 4, of which 4 were waited for; matrix products, arithmetic and copies ran while one was open for 9% of the time, Pallas kernels for 0%

commit v1 on v0

--- a/solution.py
+++ b/solution.py
@@ -61,27 +61,103 @@
     return result.astype(jnp.bfloat16).reshape(seqs * 2, HEADS * HEAD_DIM)
 
 
+def swap(value, axis, flip):
+    size = lax.axis_size(axis)
+    return lax.ppermute(value, axis, [(i, i ^ flip) for i in range(size)])
+
+
+def inner_size(size):
+    return 2 ** ((size.bit_length() - 1) // 2)
+
+
+def gather_blocks(block, axis):
+    size = lax.axis_size(axis)
+    inner = inner_size(size)
+    blocks = {0: block}
+    for outer in range(size - inner, 0, -inner):
+        blocks[outer] = swap(block, axis, outer)
+    for outer in range(0, size, inner):
+        for flip in range(1, inner):
+            blocks[outer + flip] = swap(blocks[outer], axis, flip)
+    return [blocks[k] for k in range(size)]
+
+
+def scatter_sum(parts, axis, inner, wire):
+    size = lax.axis_size(axis)
+    kept = {}
+    for outer in range(size - inner, -1, -inner):
+        total = parts[outer]
+        for flip in range(1, inner):
+            got = swap(parts[outer + flip].astype(wire), axis, flip)
+            total = total + got.astype(jnp.float32)
+        kept[outer] = total
+    total = kept[0]
+    for outer in range(inner, size, inner):
+        total = total + swap(kept[outer].astype(wire), axis, outer).astype(jnp.float32)
+    return total
+
+
+def token_rows(flat_ids, embedding, order):
+    tokens = flat_ids.shape[0]
+    span, width = embedding.shape
+    size = lax.axis_size("gy")
+    me = lax.axis_index("gy")
+    room = -(-3 * tokens // (2 * size) // 8) * 8
+    owner = flat_ids // span
+    at = jnp.arange(tokens, dtype=jnp.int32)
+    before = (owner[:, None] == owner[None, :]) & (at[None, :] < at[:, None])
+    rank = jnp.sum(before.astype(jnp.int32), axis=1)
+    local = jnp.where(owner == me, flat_ids - me * span, 0)
+    slot_of = jnp.where(owner == me, rank, -1)
+    place = (owner ^ me) * room
+    slot = jnp.arange(room, dtype=jnp.int32)
+    column = jnp.arange(room * size, dtype=jnp.int32)
+    place_o = jnp.take(place, order, axis=0)
+    rank_o = jnp.take(rank, order, axis=0)
+
+    def one_round(base):
+        mine = (slot_of[None, :] - base) == slot[:, None]
+        rows = jnp.sum(jnp.where(mine, local[None, :], 0), axis=1)
+        block = jnp.take(embedding, rows, axis=0, mode="clip")
+        everything = jnp.concatenate(gather_blocks(block, "gy"), axis=0)
+        offset = rank_o - base
+        index = jnp.where((offset >= 0) & (offset < room), place_o + offset, -1)
+        pick = (index[:, None] == column[None, :]).astype(embedding.dtype)
+        return jnp.dot(pick, everything, preferred_element_type=jnp.float32).astype(embedding.dtype)
+
+    most = jnp.max(rank) + 1
+    first = one_round(0)
+
+    def more(state):
+        return state[0] < most
+
+    def again(state):
+        return state[0] + room, state[1] + one_round(state[0])
+
+    return lax.while_loop(more, again, (jnp.int32(room), first))[1]
+
+
 def on_device(
     token_ids, lengths, embedding, norm_gain, qkv_weight, out_weight, key_cache, value_cache
 ):
     flat_ids = token_ids.reshape(-1)
-    span = embedding.shape[0]
-    local_ids = flat_ids - lax.axis_index("gy") * span
-    inside = (local_ids >= 0) & (local_ids < span)
-    picked = jnp.take(embedding, jnp.clip(local_ids, 0, span - 1), axis=0)
-    picked = jnp.where(inside[:, None], picked, jnp.zeros((), picked.dtype))
-    feature_cols = lax.psum(picked, "gy").astype(jnp.float32)
-    power = jnp.sum(feature_cols * feature_cols, axis=1)
-    scaled = (feature_cols * norm_gain[None, :]).astype(jnp.bfloat16)
-    share = feature_cols.shape[0] // lax.axis_size("gx")
-    total_power = lax.psum(power, "gx")
-    summed = lax.psum_scatter(
-        jnp.dot(scaled, qkv_weight, preferred_element_type=jnp.float32),
-        "gx",
-        scatter_dimension=0,
-        tiled=True,
-    )
-    my_power = lax.dynamic_slice_in_dim(total_power, lax.axis_index("gx") * share, share, 0)
+    tokens = flat_ids.shape[0]
+    gx, gy = lax.axis_size("gx"), lax.axis_size("gy")
+    my_x, my_y = lax.axis_index("gx"), lax.axis_index("gy")
+    share = tokens // gx
+    at = jnp.arange(tokens, dtype=jnp.int32)
+    order = ((at // share) ^ my_x) * share + at % share
+    features = token_rows(flat_ids, embedding, order)
+    wide = features.astype(jnp.float32)
+    power = jnp.sum(wide * wide, axis=1)
+    scaled = (wide * norm_gain[None, :]).astype(jnp.bfloat16)
+    partial = jnp.dot(scaled, qkv_weight, preferred_element_type=jnp.float32)
+    my_power = scatter_sum(
+        [power[k * share : (k + 1) * share] for k in range(gx)], "gx", 2, jnp.float32
+    )
+    summed = scatter_sum(
+        [partial[k * share : (k + 1) * share] for k in range(gx)], "gx", 2, jnp.bfloat16
+    )
     qkv_rows = (summed * lax.rsqrt(my_power / D + EPS)[:, None]).astype(jnp.bfloat16)
     qkv_local = lax.all_to_all(qkv_rows, "gy", split_axis=0, concat_axis=1, tiled=True)
     seqs = lengths.shape[0]
@@ -94,14 +170,26 @@
     keys_r = rotate(keys, positions).astype(jnp.bfloat16)
     attended = attend(query_r, keys_r, vals, key_cache, value_cache, lengths)
     column_block = lax.all_to_all(attended, "gy", split_axis=1, concat_axis=0, tiled=True)
-    partial_out = jnp.dot(
-        lax.all_gather(column_block, "gx", axis=0, tiled=True),
-        out_weight,
-        preferred_element_type=jnp.float32,
-    )
-    projected = lax.psum_scatter(partial_out, "gy", scatter_dimension=0, tiled=True)
-    mine = projected.shape[0]
-    residual = lax.dynamic_slice_in_dim(feature_cols, lax.axis_index("gy") * mine, mine, 0)
+    lhs = lax.all_gather(column_block, "gx", axis=0, tiled=True)
+    mine = tokens // gy
+    inner = inner_size(gy)
+    outs = [None] * gy
+    half = max(gy // 2, inner)
+    for low in range(gy - half, -1, -half):
+        block = jnp.concatenate(
+            [
+                lax.dynamic_slice_in_dim(lhs, (my_y ^ k) * mine, mine, 0)
+                for k in range(low, low + half)
+            ],
+            axis=0,
+        )
+        product = jnp.dot(block, out_weight, preferred_element_type=jnp.float32)
+        for k in range(half):
+            outs[low + k] = product[k * mine : (k + 1) * mine]
+    projected = scatter_sum(outs, "gy", inner, jnp.bfloat16)
+    first = my_y * mine
+    start = ((first // share) ^ my_x) * share + first % share
+    residual = lax.dynamic_slice_in_dim(features, start, mine, 0).astype(jnp.float32)
     layer_out = (
         (residual + projected).astype(jnp.bfloat16).reshape(mine // 2, 2, projected.shape[1])
     )

time: 294 us -> 155 us (0.53)
  waiting for transfers between devices: 171 us -> 53.5 us
  starting transfers between devices: 5.83 us -> 29.4 us
  blocking collectives: 27 us -> 8.76 us
  local copies, waits for them, and re-layouts: 46.8 us -> 33.5 us
  between operations: 14.1 us -> 1.79 us
    psum x1 -> x0, waiting for transfers between devices: 92.2 us -> none  [on_device(): feature_cols = lax.psum(picked, 'gy').astype(jnp.float32)]
    reduce_scatter x2 -> x0, waiting for transfers between devices: 74.1 us -> none  [the longest x1 70 us: on_device(): lax.psum_scatter(partial_out, 'gy', scatter_dimension=0, tiled=True)]
    ppermute x0 -> x20, waiting for transfers between devices: none -> 41.3 us  [swap(): return lax.ppermute(value, axis, [(i, i ^ flip) for i in range(size)])]
    ppermute x0 -> x20, starting transfers between devices: none -> 21.4 us  [swap(): return lax.ppermute(value, axis, [(i, i ^ flip) for i in range(size)])]
    all_to_all x1 -> x0, blocking collectives: 11.9 us -> none  [on_device(): lax.all_to_all(attended, 'gy', split_axis=1, concat_axis=0, tiled=True)]
    gather x1 -> x3, local copies, waits for them, and re-layouts: 19.8 us -> 10.5 us  [the longest x1 4.91 us: one_round(): block = jnp.take(embedding, rows, axis=0, mode='clip')]
    all_to_all x0 -> x1, waiting for transfers between devices: none -> 8.47 us  [on_device(): lax.all_to_all(attended, 'gy', split_axis=1, concat_axis=0, tiled=True)]
    psum x1 -> x0, blocking collectives: 7.4 us -> none  [on_device(): total_power = lax.psum(power, 'gx')]
  transfers between devices with their start and end apart: 4 -> 22, of which waited for: 4 -> 11; matrix products, arithmetic and copies ran while one was open for 9% -> 21% of each run, Pallas kernels for 0% -> 0%
where the time goes in v1:
time: 155 us; the launch traced here: 153 us
  waiting for transfers between devices  53.5 us (35%)
  local copies, waits for them, and re-layouts  33.5 us (22%)
  starting transfers between devices  29.4 us (19%)
  matrix products  18.2 us (12%)
  blocking collectives  8.76 us (6%)
  other arithmetic  8.14 us (5%)
  between operations  1.79 us (1%)
    ppermute x20, waiting for transfers between devices, swap(): return lax.ppermute(value, axis, [(i, i ^ flip) for i in range(size)])  41.3 us
    ppermute x20, starting transfers between devices, swap(): return lax.ppermute(value, axis, [(i, i ^ flip) for i in range(size)])  21.4 us
    unnamed x31, local copies, waits for them, and re-layouts  9.11 us
    all_gather x1, blocking collectives, on_device(): lhs = lax.all_gather(column_block, 'gx', axis=0, tiled=True)  8.76 us
    all_to_all x1, waiting for transfers between devices, on_device(): lax.all_to_all(attended, 'gy', split_axis=1, concat_axis=0, tiled=True)  8.47 us
    reshape x1, local copies, waits for them, and re-layouts, attend(): vals_c = vals_old.reshape(seqs, slots, KV_HEADS, HEAD_DIM)  5.81 us
    gather x1, local copies, waits for them, and re-layouts, one_round(): block = jnp.take(embedding, rows, axis=0, mode='clip')  4.91 us
    dot_general x1, matrix products, attend(): jnp.einsum('stghd,scgd->sgthc', query_g, keys_c, preferred_element_type=j...  4.88 us
  transfers between devices with their start and end apart: 22, of which 11 were waited for; matrix products, arithmetic and copies ran while one was open for 21% of the time, Pallas kernels for 0%

profile of v1, /device:TPU:0, one launch (start us, length us, event | category | flops | bytes accessed | tf_op | source)
XLA Modules:
  0.0 153.4 jit_solution(6136208637738309862)
XLA Ops:
  3.9 4.9 %gather_fusion.1 = bf16[72,2048]{1,0:T(8,128)(2,1)S(1)} fusion(bf16[8016,2048]{1,0:T(8,128)(2,1)} %param.14, s32[1024]{0:T(1024)S(1)} %pad_clamp_fusion.1), kind=kCustom, calls=%fused_computation.3 | custom fusion | bytes 590112 | tf_op jit(solution)/shard_map/jit(_take)/gather | solution.py:121
  8.9 3.2 %collective-permute-start.7 = (bf16[72,2048]{1,0:T(8,128)(2,1)S(1)}, bf16[72,2048]{1,0:T(8,128)(2,1)S(1)}, u32[]{:S(2)}, u32[]{:S(2)}) collective-permute-start(bf16[72,2048]{1,0:T(8,128)(2,1)S(1)} %gather_fusion.1), channel_id=1, source_target_pairs={{0,1},{1,0},{2,3},{3,2},{4,5},{5,4},{6,7},{7,6},{8,9},{9,8},{10,11... | collective-permute-start | bytes 884744 | tf_op jit(solution)/shard_map/ppermute | solution.py:66
  12.1 1.5 collective-permute-start.8
  13.6 1.9 %collective-permute-start.10 = (bf16[72,2048]{1,0:T(8,128)(2,1)S(1)}, bf16[72,2048]{1,0:T(8,128)(2,1)S(1)}, u32[]{:S(2)}, u32[]{:S(2)}) collective-permute-start(bf16[72,2048]{1,0:T(8,128)(2,1)S(1)} %gather_fusion.1), channel_id=1, source_target_pairs={{0,4},{1,5},{2,6},{3,7},{4,0},{5,1},{6,2},{7,3},{8,12},{9,13},{10,... | collective-permute-start | bytes 884744 | tf_op jit(solution)/shard_map/ppermute | solution.py:66
  16.5 2.8 %gather_fusion.2 = s32[384]{0:T(512)S(1)} fusion(s32[384]{0:T(512)S(1)} %convert_reduce_fusion, s32[1024]{0:T(1024)S(1)} %pad_clamp_fusion.2), kind=kCustom, calls=%fused_computation.clone | custom fusion | bytes 4608 | tf_op jit(solution)/shard_map/jit(_take)/gather | solution.py:116
  19.3 2.8 %gather_fusion.3 = s32[384]{0:T(512)S(1)} fusion(s32[384]{0:T(512)S(1)} %get-tuple-element.97, s32[1024]{0:T(1024)S(1)} %pad_clamp_fusion.2), kind=kCustom, calls=%fused_computation.2.clone | custom fusion | bytes 4608 | tf_op jit(solution)/shard_map/jit(_take)/gather | solution.py:115
  22.2 4.4 %copy.69 = bf16[384,8,8,128]{3,2,1,0:T(8,128)(2,1)S(1)} copy(bf16[384,8,8,128]{3,1,2,0:T(8,128)(2,1)} %bitcast.75) | data formatting | bytes 12582912
  26.6 3.0 %bitcast_bitcast_fusion.1 = bf16[6,512,8,128,1]{3,2,1,0,4:T(8,128)(2,1)} fusion(bf16[6,512,8,128]{3,2,1,0:T(8,128)(2,1)S(1)} %bitcast.74), kind=kLoop, calls=%fused_computation.24 | loop fusion | bytes 12582912 | tf_op jit(solution)/shard_map/reshape | solution.py:34
  30.7 6.3 %collective-permute-done.10 = bf16[72,2048]{1,0:T(8,128)(2,1)S(1)} collective-permute-done((bf16[72,2048]{1,0:T(8,128)(2,1)S(1)}, bf16[72,2048]{1,0:T(8,128)(2,1)S(1)}, u32[]{:S(2)}, u32[]{:S(2)}) %collective-permute-start.10) | collective-permute-done | bytes 294944 | tf_op jit(solution)/shard_map/ppermute | solution.py:66
  37.2 1.8 %collective-permute-start.13 = (bf16[72,2048]{1,0:T(8,128)(2,1)S(1)}, bf16[72,2048]{1,0:T(8,128)(2,1)S(1)}, u32[]{:S(2)}, u32[]{:S(2)}) collective-permute-start(bf16[72,2048]{1,0:T(8,128)(2,1)S(1)} %collective-permute-done.12), channel_id=1, source_target_pairs={{0,1},{1,0},{2,3},{3,2},{4,5},{5,4},{6,7},{7,6},{8,9},{9,8},{10,11... | collective-permute-start | bytes 884744 | tf_op jit(solution)/shard_map/ppermute | solution.py:66
  40.5 6.3 %collective-permute-done.11 = bf16[72,2048]{1,0:T(8,128)(2,1)S(1)} collective-permute-done((bf16[72,2048]{1,0:T(8,128)(2,1)S(1)}, bf16[72,2048]{1,0:T(8,128)(2,1)S(1)}, u32[]{:S(2)}, u32[]{:S(2)}) %collective-permute-start.11) | collective-permute-done | bytes 294944 | tf_op jit(solution)/shard_map/ppermute | solution.py:66
  46.9 3.9 %collective-permute-done.13 = bf16[72,2048]{1,0:T(8,128)(2,1)S(1)} collective-permute-done((bf16[72,2048]{1,0:T(8,128)(2,1)S(1)}, bf16[72,2048]{1,0:T(8,128)(2,1)S(1)}, u32[]{:S(2)}, u32[]{:S(2)}) %collective-permute-start.13) | collective-permute-done | bytes 294944 | tf_op jit(solution)/shard_map/ppermute | solution.py:66
  50.9 1.4 convolution_convert_fusion.1
  53.1 4.8 %fusion.86 = (bf16[384,1280]{1,0:T(8,128)(2,1)S(1)}, f32[384,1280]{1,0:T(8,128)S(1)}) fusion(bf16[2048,1280]{1,0:T(8,128)(2,1)} %param.16, bf16[384,2048]{1,0:T(8,128)(2,1)S(1)} %get-tuple-element.57, f32[2048]{0:T(1024)S(1)} %copy-done.2), kind=kOutput, calls=%fused_computation.169 | convolution fusion | flops 2016116736 | bytes 9773056 | tf_op jit(solution)/shard_map/dot_general | solution.py:154
  59.0 1.5 collective-permute-start.19
  61.2 4.3 %copy.71 = bf16[384,8,8,128]{3,2,1,0:T(8,128)(2,1)} copy(bf16[384,8,8,128]{3,1,2,0:T(8,128)(2,1)S(1)} %bitcast.78) | data formatting | bytes 12582912
  65.5 2.9 %collective-permute-done.16 = bf16[96,1280]{1,0:T(8,128)(2,1)S(1)} collective-permute-done((bf16[96,1280]{1,0:T(8,128)(2,1)S(1)}, bf16[96,1280]{1,0:T(8,128)(2,1)S(1)}, u32[]{:S(2)}, u32[]{:S(2)}) %collective-permute-start.16) | collective-permute-done | bytes 245792 | tf_op jit(solution)/shard_map/ppermute | solution.py:66
  69.3 4.3 %all-to-all-start = ((bf16[8,12,1280]{2,1,0:T(8,128)(2,1)}), bf16[8,12,1280]{2,1,0:T(8,128)(2,1)S(1)}, u32[]{:S(2)}, u32[]{:S(2)}) async-start(bf16[8,12,1280]{2,1,0:T(8,128)(2,1)} %all_to_all.28), calls=%async_computation | async-start | bytes 655360 | tf_op jit(solution)/shard_map/all_to_all | solution.py:162
  73.6 5.8 %bitcast_bitcast_fusion = bf16[6,512,8,128,1]{3,2,1,0,4:T(8,128)(2,1)} fusion(bf16[6,512,8,128]{3,2,1,0:T(8,128)(2,1)} %bitcast.73), kind=kLoop, calls=%fused_computation.23 | loop fusion | bytes 12582912 | tf_op jit(solution)/shard_map/reshape | solution.py:35
  79.4 3.7 %all-to-all-done = bf16[8,12,1280]{2,1,0:T(8,128)(2,1)S(1)} async-done(((bf16[8,12,1280]{2,1,0:T(8,128)(2,1)}), bf16[8,12,1280]{2,1,0:T(8,128)(2,1)S(1)}, u32[]{:S(2)}, u32[]{:S(2)}) %all-to-all-start) | async-done | bytes 245792 | tf_op jit(solution)/shard_map/all_to_all | solution.py:162
  83.9 4.9 %fusion.87 = (f32[6,8,2,8]{3,2,1,0:T(2,128)S(1)}, f32[6,8,2,8,512]{4,3,2,1,0:T(8,128)S(1)}) fusion(bf16[6,512,8,128,1]{3,2,1,0,4:T(8,128)(2,1)} %bitcast_bitcast_fusion.1, pred[6,512]{1,0:T(8,128)(4,1)S(1)} %iota_compare_fusion.7, bf16[6,2,8,8,64]{4,3,2,1,0:T(8,128)(2,1)S(1)} %get-tuple-element.118, bf16[6,2,8,8,64]{4,3,2,1,0:T(8,128)(2,1)S(1)} %get-tuple-element.117), kind=kOutput, calls=%fused_computation.170 | convolution fusion | flops 102235392 | bytes 8067072 | tf_op jit(solution)/shard_map/stghd,scgd->sgthc/dot_general | solution.py:37
  93.2 3.6 %all-to-all-start.1 = ((bf16[12,8,1024]{2,0,1:T(8,128)(2,1)}), bf16[12,8,1024]{2,0,1:T(8,128)(2,1)S(1)}, u32[]{:S(2)}, u32[]{:S(2)}) async-start(bf16[12,8,1024]{2,0,1:T(8,128)(2,1)} %reshape.272), calls=%async_computation.1 | async-start | bytes 524288 | tf_op jit(solution)/shard_map/all_to_all | solution.py:172
  96.9 8.5 %all-to-all-done.1 = bf16[12,8,1024]{2,0,1:T(8,128)(2,1)S(1)} async-done(((bf16[12,8,1024]{2,0,1:T(8,128)(2,1)}), bf16[12,8,1024]{2,0,1:T(8,128)(2,1)S(1)}, u32[]{:S(2)}, u32[]{:S(2)}) %all-to-all-start.1) | async-done | bytes 196640 | tf_op jit(solution)/shard_map/all_to_all | solution.py:172
  105.4 8.8 %all_gather.3 = bf16[384,1024]{1,0:T(8,128)(2,1)S(1)} all-gather(bf16[96,1024]{1,0:T(8,128)(2,1)S(1)} %all_to_all.35), channel_id=1, replica_groups=mesh['gx'=4,'gy'=8] {'gx'}, dimensions={0}, use_global_device_ids=true | all-gather | bytes 983040 | tf_op jit(solution)/shard_map/all_gather | solution.py:173
  114.2 3.3 %fusion.90 = (bf16[192,2048]{1,0:T(8,128)(2,1)S(1)}, f32[192,2048]{1,0:T(8,128)S(1)}) fusion(bf16[1024,2048]{1,0:T(8,128)(2,1)} %param.17, bf16[48,1024]{1,0:T(8,128)(2,1)S(1)} %get-tuple-element.113, bf16[48,1024]{1,0:T(8,128)(2,1)S(1)} %get-tuple-element.114, bf16[48,1024]{1,0:T(8,128)(2,1)S(1)} %get-tuple-element.115, ...), kind=kOutput, calls=%fused_computation.173 | convolution fusion | flops 807272448 | bytes 6946816 | tf_op jit(solution)/shard_map/dot_general | solution.py:186
  118.3 1.4 collective-permute-start.21
  121.4 1.4 collective-permute-start.25
  123.4 2.6 %collective-permute-done.21 = bf16[48,2048]{1,0:T(8,128)(2,1)S(1)} collective-permute-done((bf16[48,2048]{1,0:T(8,128)(2,1)S(1)}, bf16[48,2048]{1,0:T(8,128)(2,1)S(1)}, u32[]{:S(2)}, u32[]{:S(2)}) %collective-permute-start.21) | collective-permute-done | bytes 196640 | tf_op jit(solution)/shard_map/ppermute | solution.py:66
  127.8 2.4 %collective-permute-done.23 = bf16[48,2048]{1,0:T(8,128)(2,1)S(1)} collective-permute-done((bf16[48,2048]{1,0:T(8,128)(2,1)S(1)}, bf16[48,2048]{1,0:T(8,128)(2,1)S(1)}, u32[]{:S(2)}, u32[]{:S(2)}) %collective-permute-start.23) | collective-permute-done | bytes 196640 | tf_op jit(solution)/shard_map/ppermute | solution.py:66
  130.3 4.2 %collective-permute-done.25 = bf16[48,2048]{1,0:T(8,128)(2,1)S(1)} collective-permute-done((bf16[48,2048]{1,0:T(8,128)(2,1)S(1)}, bf16[48,2048]{1,0:T(8,128)(2,1)S(1)}, u32[]{:S(2)}, u32[]{:S(2)}) %collective-permute-start.25) | collective-permute-done | bytes 196640 | tf_op jit(solution)/shard_map/ppermute | solution.py:66
  136.3 2.4 %collective-permute-start.26 = (bf16[48,2048]{1,0:T(8,128)(2,1)S(1)}, bf16[48,2048]{1,0:T(8,128)(2,1)}, u32[]{:S(2)}, u32[]{:S(2)}) collective-permute-start(bf16[48,2048]{1,0:T(8,128)(2,1)S(1)} %get-tuple-element.102), channel_id=1, source_target_pairs={{0,6},{1,7},{2,4},{3,5},{4,2},{5,3},{6,0},{7,1},{8,14},{9,15},{10,... | collective-permute-start | bytes 589832 | tf_op jit(solution)/shard_map/ppermute | solution.py:66
  140.0 11.2 %collective-permute-done.24 = bf16[48,2048]{1,0:T(8,128)(2,1)} collective-permute-done((bf16[48,2048]{1,0:T(8,128)(2,1)}, bf16[48,2048]{1,0:T(8,128)(2,1)}, u32[]{:S(2)}, u32[]{:S(2)}) %collective-permute-start.24) | collective-permute-done | bytes 196640 | tf_op jit(solution)/shard_map/ppermute | solution.py:66
  (113 shorter events, 25.2 us)
Async XLA Ops:
  8.8 13.3 %copy-start.1 = (s32[6]{0:T(128)S(1)}, s32[6]{0:T(128)}, u32[]{:S(2)}) copy-start(s32[6]{0:T(128)} %param.13) | copy-start | bytes 76
  8.9 30.2 %collective-permute-start.7 = (bf16[72,2048]{1,0:T(8,128)(2,1)S(1)}, bf16[72,2048]{1,0:T(8,128)(2,1)S(1)}, u32[]{:S(2)}, u32[]{:S(2)}) collective-permute-start(bf16[72,2048]{1,0:T(8,128)(2,1)S(1)} %gather_fusion.1), channel_id=1, source_target_pairs={{0,1},{1,0},{2,3},{3,2},{4,5},{5,4},{6,7},{7,6},{8,9},{9,8},{10,11... | collective-permute-start | bytes 884744 | tf_op jit(solution)/shard_map/ppermute | solution.py:66
  12.1 18.4 %collective-permute-start.8 = (bf16[72,2048]{1,0:T(8,128)(2,1)S(1)}, bf16[72,2048]{1,0:T(8,128)(2,1)S(1)}, u32[]{:S(2)}, u32[]{:S(2)}) collective-permute-start(bf16[72,2048]{1,0:T(8,128)(2,1)S(1)} %gather_fusion.1), channel_id=1, source_target_pairs={{0,2},{1,3},{2,0},{3,1},{4,6},{5,7},{6,4},{7,5},{8,10},{9,11},{10,... | collective-permute-start | bytes 884744 | tf_op jit(solution)/shard_map/ppermute | solution.py:66
  13.6 23.4 %collective-permute-start.10 = (bf16[72,2048]{1,0:T(8,128)(2,1)S(1)}, bf16[72,2048]{1,0:T(8,128)(2,1)S(1)}, u32[]{:S(2)}, u32[]{:S(2)}) collective-permute-start(bf16[72,2048]{1,0:T(8,128)(2,1)S(1)} %gather_fusion.1), channel_id=1, source_target_pairs={{0,4},{1,5},{2,6},{3,7},{4,0},{5,1},{6,2},{7,3},{8,12},{9,13},{10,... | collective-permute-start | bytes 884744 | tf_op jit(solution)/shard_map/ppermute | solution.py:66
  15.4 21.8 %collective-permute-start.12 = (bf16[72,2048]{1,0:T(8,128)(2,1)S(1)}, bf16[72,2048]{1,0:T(8,128)(2,1)S(1)}, u32[]{:S(2)}, u32[]{:S(2)}) collective-permute-start(bf16[72,2048]{1,0:T(8,128)(2,1)S(1)} %gather_fusion.1), channel_id=1, source_target_pairs={{0,6},{1,7},{2,4},{3,5},{4,2},{5,3},{6,0},{7,1},{8,14},{9,15},{10,... | collective-permute-start | bytes 884744 | tf_op jit(solution)/shard_map/ppermute | solution.py:66
  30.5 9.9 %collective-permute-start.9 = (bf16[72,2048]{1,0:T(8,128)(2,1)S(1)}, bf16[72,2048]{1,0:T(8,128)(2,1)S(1)}, u32[]{:S(2)}, u32[]{:S(2)}) collective-permute-start(bf16[72,2048]{1,0:T(8,128)(2,1)S(1)} %collective-permute-done.8), channel_id=1, source_target_pairs={{0,1},{1,0},{2,3},{3,2},{4,5},{5,4},{6,7},{7,6},{8,9},{9,8},{10,11... | collective-permute-start | bytes 884744 | tf_op jit(solution)/shard_map/ppermute | solution.py:66
  37.0 9.9 %collective-permute-start.11 = (bf16[72,2048]{1,0:T(8,128)(2,1)S(1)}, bf16[72,2048]{1,0:T(8,128)(2,1)S(1)}, u32[]{:S(2)}, u32[]{:S(2)}) collective-permute-start(bf16[72,2048]{1,0:T(8,128)(2,1)S(1)} %collective-permute-done.10), channel_id=1, source_target_pairs={{0,1},{1,0},{2,3},{3,2},{4,5},{5,4},{6,7},{7,6},{8,9},{9,8},{10,11... | collective-permute-start | bytes 884744 | tf_op jit(solution)/shard_map/ppermute | solution.py:66
  37.2 13.7 %collective-permute-start.13 = (bf16[72,2048]{1,0:T(8,128)(2,1)S(1)}, bf16[72,2048]{1,0:T(8,128)(2,1)S(1)}, u32[]{:S(2)}, u32[]{:S(2)}) collective-permute-start(bf16[72,2048]{1,0:T(8,128)(2,1)S(1)} %collective-permute-done.12), channel_id=1, source_target_pairs={{0,1},{1,0},{2,3},{3,2},{4,5},{5,4},{6,7},{7,6},{8,9},{9,8},{10,11... | collective-permute-start | bytes 884744 | tf_op jit(solution)/shard_map/ppermute | solution.py:66
  52.3 0.7 copy-start.2
  53.0 8.1 %slice-start.2 = ((s8[6291456]{0:T(1024)(128)(4,1)}), s8[4194304]{0:T(1024)(128)(4,1)S(1)}, s32[]{:S(2)}) async-start(s8[6291456]{0:T(1024)(128)(4,1)} %bitcast.76), calls=%async_computation.4 | async-start | bytes 8388608
  53.0 8.1 %slice-start.3 = ((s8[6291456]{0:T(1024)(128)(4,1)}), s8[2097152]{0:T(1024)(128)(4,1)S(1)}, s32[]{:S(2)}) async-start(s8[6291456]{0:T(1024)(128)(4,1)} %bitcast.76), calls=%async_computation.5 | async-start | bytes 4194304
  53.0 5.9 %collective-permute-start.18 = (f32[96]{0:T(128)S(1)}, f32[96]{0:T(128)S(1)}, u32[]{:S(2)}, u32[]{:S(2)}) collective-permute-start(f32[96]{0:T(128)S(1)} %get-tuple-element.128), channel_id=1, source_target_pairs={{0,8},{8,0},{16,24},{24,16},{1,9},{9,1},{17,25},{25,17},{2,10},{10... | collective-permute-start | bytes 1160 | tf_op jit(solution)/shard_map/ppermute | solution.py:66
  57.9 2.6 %collective-permute-start.15 = (bf16[96,1280]{1,0:T(8,128)(2,1)S(1)}, bf16[96,1280]{1,0:T(8,128)(2,1)S(1)}, u32[]{:S(2)}, u32[]{:S(2)}) collective-permute-start(bf16[96,1280]{1,0:T(8,128)(2,1)S(1)} %get-tuple-element.104), channel_id=1, source_target_pairs={{0,8},{8,0},{16,24},{24,16},{1,9},{9,1},{17,25},{25,17},{2,10},{10... | collective-permute-start | bytes 737288 | tf_op jit(solution)/shard_map/ppermute | solution.py:66
  58.4 7.0 %collective-permute-start.17 = (f32[96]{0:T(128)S(1)}, f32[96]{0:T(128)S(1)}, u32[]{:S(2)}, u32[]{:S(2)}) collective-permute-start(f32[96]{0:T(128)S(1)} %get-tuple-element.127), channel_id=1, source_target_pairs={{0,8},{8,0},{16,24},{24,16},{1,9},{9,1},{17,25},{25,17},{2,10},{10... | collective-permute-start | bytes 1160 | tf_op jit(solution)/shard_map/ppermute | solution.py:66
  58.6 6.9 %collective-permute-start.14 = (bf16[96,1280]{1,0:T(8,128)(2,1)S(1)}, bf16[96,1280]{1,0:T(8,128)(2,1)S(1)}, u32[]{:S(2)}, u32[]{:S(2)}) collective-permute-start(bf16[96,1280]{1,0:T(8,128)(2,1)S(1)} %get-tuple-element.103), channel_id=1, source_target_pairs={{0,8},{8,0},{16,24},{24,16},{1,9},{9,1},{17,25},{25,17},{2,10},{10... | collective-permute-start | bytes 737288 | tf_op jit(solution)/shard_map/ppermute | solution.py:66
  59.0 6.4 %collective-permute-start.19 = (f32[96]{0:T(128)S(1)}, f32[96]{0:T(128)S(1)}, u32[]{:S(2)}, u32[]{:S(2)}) collective-permute-start(f32[96]{0:T(128)S(1)} %slice_add_fusion.6), channel_id=1, source_target_pairs={{0,16},{8,24},{16,0},{24,8},{1,17},{9,25},{17,1},{25,9},{2,18},{10... | collective-permute-start | bytes 1160 | tf_op jit(solution)/shard_map/ppermute | solution.py:66
  60.6 7.8 %collective-permute-start.16 = (bf16[96,1280]{1,0:T(8,128)(2,1)S(1)}, bf16[96,1280]{1,0:T(8,128)(2,1)S(1)}, u32[]{:S(2)}, u32[]{:S(2)}) collective-permute-start(bf16[96,1280]{1,0:T(8,128)(2,1)S(1)} %fusion.29), channel_id=1, source_target_pairs={{0,16},{8,24},{16,0},{24,8},{1,17},{9,25},{17,1},{25,9},{2,18},{10... | collective-permute-start | bytes 737288 | tf_op jit(solution)/shard_map/ppermute | solution.py:66
  69.3 13.8 %all-to-all-start = ((bf16[8,12,1280]{2,1,0:T(8,128)(2,1)}), bf16[8,12,1280]{2,1,0:T(8,128)(2,1)S(1)}, u32[]{:S(2)}, u32[]{:S(2)}) async-start(bf16[8,12,1280]{2,1,0:T(8,128)(2,1)} %all_to_all.28), calls=%async_computation | async-start | bytes 655360 | tf_op jit(solution)/shard_map/all_to_all | solution.py:162
  83.9 6.8 %slice-start = ((s8[6291456]{0:T(1024)(128)(4,1)}), s8[4194304]{0:T(1024)(128)(4,1)S(1)}, s32[]{:S(2)}) async-start(s8[6291456]{0:T(1024)(128)(4,1)} %bitcast.71), calls=%async_computation.2 | async-start | bytes 8388608
  83.9 6.8 %slice-start.1 = ((s8[6291456]{0:T(1024)(128)(4,1)}), s8[2097152]{0:T(1024)(128)(4,1)S(1)}, s32[]{:S(2)}) async-start(s8[6291456]{0:T(1024)(128)(4,1)} %bitcast.71), calls=%async_computation.3 | async-start | bytes 4194304
  93.2 12.1 %all-to-all-start.1 = ((bf16[12,8,1024]{2,0,1:T(8,128)(2,1)}), bf16[12,8,1024]{2,0,1:T(8,128)(2,1)S(1)}, u32[]{:S(2)}, u32[]{:S(2)}) async-start(bf16[12,8,1024]{2,0,1:T(8,128)(2,1)} %reshape.272), calls=%async_computation.1 | async-start | bytes 524288 | tf_op jit(solution)/shard_map/all_to_all | solution.py:172
  114.2 5.5 %copy-start = (bf16[1024,2048]{1,0:T(8,128)(2,1)S(1)}, bf16[1024,2048]{1,0:T(8,128)(2,1)}, u32[]{:S(2)}) copy-start(bf16[1024,2048]{1,0:T(8,128)(2,1)} %param.17) | copy-start | bytes 12582916
  118.3 7.8 %collective-permute-start.21 = (bf16[48,2048]{1,0:T(8,128)(2,1)S(1)}, bf16[48,2048]{1,0:T(8,128)(2,1)S(1)}, u32[]{:S(2)}, u32[]{:S(2)}) collective-permute-start(bf16[48,2048]{1,0:T(8,128)(2,1)S(1)} %get-tuple-element.106), channel_id=1, source_target_pairs={{0,1},{1,0},{2,3},{3,2},{4,5},{5,4},{6,7},{7,6},{8,9},{9,8},{10,11... | collective-permute-start | bytes 589832 | tf_op jit(solution)/shard_map/ppermute | solution.py:66
  120.7 9.5 %collective-permute-start.23 = (bf16[48,2048]{1,0:T(8,128)(2,1)S(1)}, bf16[48,2048]{1,0:T(8,128)(2,1)S(1)}, u32[]{:S(2)}, u32[]{:S(2)}) collective-permute-start(bf16[48,2048]{1,0:T(8,128)(2,1)S(1)} %get-tuple-element.107), channel_id=1, source_target_pairs={{0,1},{1,0},{2,3},{3,2},{4,5},{5,4},{6,7},{7,6},{8,9},{9,8},{10,11... | collective-permute-start | bytes 589832 | tf_op jit(solution)/shard_map/ppermute | solution.py:66
  121.4 13.1 %collective-permute-start.25 = (bf16[48,2048]{1,0:T(8,128)(2,1)S(1)}, bf16[48,2048]{1,0:T(8,128)(2,1)S(1)}, u32[]{:S(2)}, u32[]{:S(2)}) collective-permute-start(bf16[48,2048]{1,0:T(8,128)(2,1)S(1)} %get-tuple-element.108), channel_id=1, source_target_pairs={{0,1},{1,0},{2,3},{3,2},{4,5},{5,4},{6,7},{7,6},{8,9},{9,8},{10,11... | collective-permute-start | bytes 589832 | tf_op jit(solution)/shard_map/ppermute | solution.py:66
  122.8 17.2 %collective-permute-start.20 = (bf16[48,2048]{1,0:T(8,128)(2,1)}, bf16[48,2048]{1,0:T(8,128)(2,1)}, u32[]{:S(2)}, u32[]{:S(2)}) collective-permute-start(bf16[48,2048]{1,0:T(8,128)(2,1)} %get-tuple-element.105), channel_id=1, source_target_pairs={{0,1},{1,0},{2,3},{3,2},{4,5},{5,4},{6,7},{7,6},{8,9},{9,8},{10,11... | collective-permute-start | bytes 589832 | tf_op jit(solution)/shard_map/ppermute | solution.py:66
  126.8 13.3 %collective-permute-start.22 = (bf16[48,2048]{1,0:T(8,128)(2,1)}, bf16[48,2048]{1,0:T(8,128)(2,1)}, u32[]{:S(2)}, u32[]{:S(2)}) collective-permute-start(bf16[48,2048]{1,0:T(8,128)(2,1)} %fusion.36), channel_id=1, source_target_pairs={{0,2},{1,3},{2,0},{3,1},{4,6},{5,7},{6,4},{7,5},{8,10},{9,11},{10,... | collective-permute-start | bytes 589832 | tf_op jit(solution)/shard_map/ppermute | solution.py:66
  135.2 15.9 %collective-permute-start.24 = (bf16[48,2048]{1,0:T(8,128)(2,1)}, bf16[48,2048]{1,0:T(8,128)(2,1)}, u32[]{:S(2)}, u32[]{:S(2)}) collective-permute-start(bf16[48,2048]{1,0:T(8,128)(2,1)} %get-tuple-element.101), channel_id=1, source_target_pairs={{0,4},{1,5},{2,6},{3,7},{4,0},{5,1},{6,2},{7,3},{8,12},{9,13},{10,... | collective-permute-start | bytes 589832 | tf_op jit(solution)/shard_map/ppermute | solution.py:66
  136.3 14.9 %collective-permute-start.26 = (bf16[48,2048]{1,0:T(8,128)(2,1)S(1)}, bf16[48,2048]{1,0:T(8,128)(2,1)}, u32[]{:S(2)}, u32[]{:S(2)}) collective-permute-start(bf16[48,2048]{1,0:T(8,128)(2,1)S(1)} %get-tuple-element.102), channel_id=1, source_target_pairs={{0,6},{1,7},{2,4},{3,5},{4,2},{5,3},{6,0},{7,1},{8,14},{9,15},{10,... | collective-permute-start | bytes 589832 | tf_op jit(solution)/shard_map/ppermute | solution.py:66
